TPU v7x, 32 devices: a whole 2x2x4 slice. The times are simulated.
32 devices in a mesh: src: 4 (over y, x), cell: 8 (over z, core).
Axes of the slice: x: 2, y: 2, z: 4, core: 2. Of those that a mesh axis runs over, the one named last changes fastest.
Arguments:
- green_source: bfloat16 [32, 8192], P('src', 'cell'), may hold values from -6 to 6
- green_receiver: bfloat16 [64, 8192], P('src', 'cell'), may hold values from -6 to 6
- pair_source: int32 [2048], P('src'), may hold values from 0 to 7
- pair_receiver: int32 [2048], P('src'), may hold values from 0 to 63
- cell_order: int32 [8, 1024], P('cell'), may hold values from 0 to 1023, each once within a row
- test_models: bfloat16 [128, 8192], P(None, 'cell'), may hold values from -6 to 6
- data_noise: bfloat16 [2048, 128], P('src'), may hold values from -8 to 8
Outputs:
- recovered: float32 [128, 8192], P('src', 'cell')
- data_residual: float32 [2048, 128], P(('src', 'cell'))
Inputs may be any that keep to these rules, and one draw needn't show every extreme that they name: Each row of cell_order holds every number of 0 to 1023 once.
All inputs are finite; a program needn't handle non-finite values.
Results may differ from a plain program's by a relative error of at most 0.012.
Values may be sent and summed in bfloat16 or wider, within the bound.
A program may use at most 64 MiB of HBM per device.

v0:
```python
import math

import jax
import jax.numpy as jnp
from jax import lax
from jax.sharding import PartitionSpec as P

HSTEPS = 2


def shards(
    green_source, green_receiver, pair_source, pair_receiver, cell_order, test_models, data_noise
):
    group_pairs = pair_source.shape[0]
    tile_cells = green_source.shape[1]
    models_count = test_models.shape[0]
    tiles_count = lax.axis_size("cell")
    share = group_pairs // tiles_count
    first_row = lax.axis_index("cell") * share
    groups_count = lax.axis_size("src")
    own_models = models_count // groups_count
    first_model = lax.axis_index("src") * own_models
    pairs_all = group_pairs * groups_count
    scale = 1.0 / math.sqrt(tile_cells * tiles_count)
    order = cell_order[0]
    receivers = lax.all_gather(green_receiver, "src", axis=0, tiled=True)
    source_cols = jnp.take(green_source, order, axis=1)
    receiver_cols = jnp.take(receivers, order, axis=1)
    kernel = (
        jnp.take(source_cols, pair_source, axis=0).astype(jnp.float32)
        * jnp.take(receiver_cols, pair_receiver, axis=0).astype(jnp.float32)
    ).astype(jnp.bfloat16)
    contract_cells = (((1,), (1,)), ((), ()))
    contract_pairs = (((0,), (0,)), ((), ()))

    def forward(models_low):
        partial_data = lax.dot_general(
            kernel, models_low, contract_cells, preferred_element_type=jnp.float32
        )
        return lax.psum(partial_data, "cell") * scale

    def pair_total(values):
        return lax.psum(values, "src")

    noise = data_noise.astype(jnp.float32)
    residual = -(forward(test_models) + noise)
    recovered = jnp.zeros((own_models, tile_cells), jnp.float32)
    for step in range(HSTEPS):
        spread = pair_total(jnp.sum(residual * residual, axis=0)[None, :])[0]
        delta = 1.0 * jnp.sqrt(spread / pairs_all + 1e-06)
        weight = delta[None, :] / jnp.maximum(jnp.abs(residual), delta[None, :])
        weighted = (weight * residual).astype(jnp.bfloat16)
        partial_grad = lax.dot_general(
            weighted, kernel, contract_pairs, preferred_element_type=jnp.float32
        )
        grad_own = (
            lax.psum_scatter(
                partial_grad.astype(jnp.bfloat16), "src", scatter_dimension=0, tiled=True
            ).astype(jnp.float32)
            * scale
        )
        grad_low = lax.all_gather(grad_own.astype(jnp.bfloat16), "src", axis=0, tiled=True)
        image = forward(grad_low)
        placed = lax.dynamic_update_slice_in_dim(
            jnp.zeros((models_count,), jnp.float32),
            jnp.sum(grad_own * grad_own, axis=1),
            first_model,
            0,
        )
        numer = lax.psum(placed, ("src", "cell"))
        totals = pair_total(jnp.sum(weight * image * image, axis=0)[None, :])
        curvature = totals[0]
        alpha = numer / (curvature + 1e-06)
        alpha_own = lax.dynamic_slice_in_dim(alpha, first_model, own_models, 0)
        recovered = recovered - alpha_own[:, None] * grad_own
        residual = residual - alpha[None, :] * image
    residual = lax.dynamic_slice_in_dim(residual, first_row, share, 0)
    return (recovered, residual)


def solution(mesh):
    return jax.shard_map(
        shards,
        mesh=mesh,
        in_specs=(
            P("src", "cell"),
            P("src", "cell"),
            P("src"),
            P("src"),
            P("cell", None),
            P(None, "cell"),
            P("src", None),
        ),
        out_specs=(P("src", "cell"), P(("src", "cell"), None)),
        check_vma=False,
    )
```

profile of v0, /device:TPU:0, one launch (start us, length us, event | category | flops | bytes accessed | tf_op | source)
XLA Modules:
  0.0 320.2 jit_solution(196052620341855435)
XLA Ops:
  7.2 0.0 copy-start
  7.2 0.0 all-reduce.4.cloned.1.call-start
  7.2 0.7 compare_select_fusion.2
  7.9 0.7 compare_select_fusion.3
  8.6 0.7 compare_and_fusion.1
  9.3 0.7 compare_select_fusion
  10.0 10.1 %all_gather.9 = bf16[64,1024]{1,0:T(8,128)(2,1)S(1)} all-gather(bf16[16,1024]{1,0:T(8,128)(2,1)} %param.8), channel_id=1, replica_groups=mesh['src'=4,'cell'=8] {'src'}, dimensions={0}, use_global_device_ids=true | all-gather | bytes 163840 | tf_op jit(solution)/shard_map/all_gather | solution.py:26
  20.1 0.2 copy.19
  20.3 0.7 compare_and_fusion
  21.0 3.2 gather_fusion.2
  24.2 0.2 select_bitcast_fusion
  24.4 0.1 copy.20
  24.6 0.0 copy-done.5
  24.6 0.2 copy.17
  24.8 3.2 %gather_fusion = bf16[1024,8]{1,0:T(8,128)(2,1)S(1)} fusion(bf16[8,1024]{0,1:T(8,128)(2,1)S(1)} %copy.17, s32[1024]{0:T(1024)S(1)} %broadcast_clamp_fusion), kind=kCustom, calls=%fused_computation | custom fusion | bytes 36864 | tf_op jit(solution)/shard_map/jit(_take)/gather | solution.py:27
  28.0 0.2 select_bitcast_fusion.1
  28.2 0.1 copy.18
  28.3 2.1 gather_fusion.3
  30.4 2.1 gather_fusion.1
  32.5 0.5 multiply_convert_fusion
  32.9 0.0 copy-done
  32.9 0.0 copy-start.2
  32.9 1.1 fusion.12
  34.1 0.0 all-reduce.4.cloned.1.call-update
  34.1 0.0 reduce-scatter.3.cloned.1.call-start
  34.2 55.3 %all-reduce.4.cloned.1.call-done = f32[512,128]{1,0:T(8,128)} async-done(((f32[512,128]{1,0:T(8,128)}), f32[512,128]{1,0:T(8,128)}) %all-reduce.4.cloned.1.call-update) | async-done | bytes 262160 | tf_op jit(solution)/shard_map/psum | solution.py:40
  89.4 0.0 copy-done.2
  89.4 1.0 multiply_reduce_fusion.1
  90.5 9.8 %psum.64 = f32[1,128]{1,0:T(1,128)S(1)} all-reduce(f32[1,128]{1,0:T(1,128)S(1)} %bitcast.34), channel_id=1, replica_groups=mesh['src'=4,'cell'=8] {'src'}, use_global_device_ids=true, to_apply=%region_2.3 | all-reduce | flops 128 | bytes 1024 | tf_op jit(solution)/shard_map/psum | solution.py:43
  100.3 2.0 convolution_convert_fusion.1
  102.3 0.0 reduce-scatter.3.cloned.1.call-update
  102.4 0.0 all-reduce.6.cloned.1.call-start
  102.4 21.4 %reduce-scatter.3.cloned.1.call-done = bf16[32,1024]{1,0:T(8,128)(2,1)} async-done(((bf16[128,1024]{1,0:T(8,128)(2,1)}), bf16[32,1024]{1,0:T(8,128)(2,1)}) %reduce-scatter.3.cloned.1.call-update) | async-done | bytes 65552 | tf_op jit(solution)/shard_map/reduce_scatter | solution.py:57
  123.8 1.0 fusion.7
  124.8 9.4 %all_gather.10 = bf16[128,1024]{1,0:T(8,128)(2,1)S(1)} all-gather(bf16[32,1024]{1,0:T(8,128)(2,1)S(1)} %get-tuple-element.11), channel_id=1, replica_groups=mesh['src'=4,'cell'=8] {'src'}, dimensions={0}, use_global_device_ids=true | all-gather | bytes 327680 | tf_op jit(solution)/shard_map/all_gather | solution.py:62
  134.2 1.2 fusion.13
  135.3 0.0 all-reduce.6.cloned.1.call-update
  135.4 0.0 reduce-scatter.5.cloned.1.call-start
  135.4 0.2 dynamic_update_slice.6
  135.7 39.3 %psum.65 = f32[128]{0:T(128)S(1)} all-reduce(f32[128]{0:T(128)S(1)} %dynamic_update_slice.6), channel_id=1, replica_groups=mesh['src'=4,'cell'=8] {'src','cell'}, use_global_device_ids=true, to_apply=%region_5.6 | all-reduce | flops 128 | bytes 1024 | tf_op jit(solution)/shard_map/psum | solution.py:70
  174.9 15.6 %all-reduce.6.cloned.1.call-done = f32[512,128]{1,0:T(8,128)} async-done(((f32[512,128]{1,0:T(8,128)}), f32[512,128]{1,0:T(8,128)}) %all-reduce.6.cloned.1.call-update) | async-done | bytes 262160 | tf_op jit(solution)/shard_map/psum | solution.py:40
  190.6 0.0 copy-done.1
  190.6 1.1 fusion
  191.6 9.8 %psum.67 = f32[1,128]{1,0:T(1,128)S(1)} all-reduce(f32[1,128]{1,0:T(1,128)S(1)} %bitcast.33), channel_id=1, replica_groups=mesh['src'=4,'cell'=8] {'src'}, use_global_device_ids=true, to_apply=%region_8.9 | all-reduce | flops 128 | bytes 1024 | tf_op jit(solution)/shard_map/psum | solution.py:43
  201.5 1.0 multiply_reduce_fusion
  202.5 8.0 %psum.68 = f32[1,128]{1,0:T(1,128)S(1)} all-reduce(f32[1,128]{1,0:T(1,128)S(1)} %bitcast.32), channel_id=1, replica_groups=mesh['src'=4,'cell'=8] {'src'}, use_global_device_ids=true, to_apply=%region_10.11 | all-reduce | flops 128 | bytes 1024 | tf_op jit(solution)/shard_map/psum | solution.py:43
  210.5 1.0 convolution_convert_fusion
  211.6 0.0 reduce-scatter.5.cloned.1.call-update
  211.6 0.0 all-reduce.8.cloned.1.call-start
  211.6 22.3 %reduce-scatter.5.cloned.1.call-done = bf16[32,1024]{1,0:T(8,128)(2,1)} async-done(((bf16[128,1024]{1,0:T(8,128)(2,1)}), bf16[32,1024]{1,0:T(8,128)(2,1)}) %reduce-scatter.5.cloned.1.call-update) | async-done | bytes 65552 | tf_op jit(solution)/shard_map/reduce_scatter | solution.py:57
  233.9 1.0 fusion.4
  234.9 9.3 %all_gather.11 = bf16[128,1024]{1,0:T(8,128)(2,1)S(1)} all-gather(bf16[32,1024]{1,0:T(8,128)(2,1)S(1)} %get-tuple-element.8), channel_id=1, replica_groups=mesh['src'=4,'cell'=8] {'src'}, dimensions={0}, use_global_device_ids=true | all-gather | bytes 327680 | tf_op jit(solution)/shard_map/all_gather | solution.py:62
  244.2 1.2 fusion.14
  245.3 0.0 all-reduce.8.cloned.1.call-update
  245.4 0.1 dynamic-slice_multiply_fusion.2
  245.5 0.2 dynamic_update_slice.7
  245.6 39.3 %psum.69 = f32[128]{0:T(128)S(1)} all-reduce(f32[128]{0:T(128)S(1)} %dynamic_update_slice.7), channel_id=1, replica_groups=mesh['src'=4,'cell'=8] {'src','cell'}, use_global_device_ids=true, to_apply=%region_13.14 | all-reduce | flops 128 | bytes 1024 | tf_op jit(solution)/shard_map/psum | solution.py:70
  285.0 15.6 %all-reduce.8.cloned.1.call-done = f32[512,128]{1,0:T(8,128)} async-done(((f32[512,128]{1,0:T(8,128)}), f32[512,128]{1,0:T(8,128)}) %all-reduce.8.cloned.1.call-update) | async-done | bytes 262160 | tf_op jit(solution)/shard_map/psum | solution.py:40
  300.5 1.0 fusion.1
  301.6 9.8 %psum.71 = f32[1,128]{1,0:T(1,128)S(1)} all-reduce(f32[1,128]{1,0:T(1,128)S(1)} %bitcast.35), channel_id=1, replica_groups=mesh['src'=4,'cell'=8] {'src'}, use_global_device_ids=true, to_apply=%region_16.17 | all-reduce | flops 128 | bytes 1024 | tf_op jit(solution)/shard_map/psum | solution.py:43
  311.4 0.1 dynamic-slice_multiply_fusion.1
  311.5 1.4 dynamic-slice_subtract_fusion
  312.9 0.0 copy-done.3
  312.9 0.7 fusion.9
  (14 shorter events, 0.1 us)
Async XLA Ops:
  7.2 25.8 %copy-start = (bf16[128,1024]{1,0:T(8,128)(2,1)S(1)}, bf16[128,1024]{1,0:T(8,128)(2,1)}, u32[]{:S(2)}) copy-start(bf16[128,1024]{1,0:T(8,128)(2,1)} %param.12) | copy-start | bytes 786436
  7.2 82.2 %all-reduce.4.cloned.1.call-start = ((), (), s32[]{:S(2)}) async-start(), calls=%async_computation.2 | async-start | bytes 524288 | tf_op jit(solution)/shard_map/psum | solution.py:40
  21.0 3.6 %copy-start.5 = (bf16[8,1024]{1,0:T(8,128)(2,1)S(1)}, bf16[8,1024]{1,0:T(8,128)(2,1)}, u32[]{:S(2)}) copy-start(bf16[8,1024]{1,0:T(8,128)(2,1)} %param.7) | copy-start | bytes 49156
  32.9 56.5 %copy-start.2 = (bf16[512,128]{1,0:T(8,128)(2,1)S(1)}, bf16[512,128]{1,0:T(8,128)(2,1)}, u32[]{:S(2)}) copy-start(bf16[512,128]{1,0:T(8,128)(2,1)} %param.13) | copy-start | bytes 393220
  34.1 89.7 %reduce-scatter.3.cloned.1.call-start = ((), (), s32[]{:S(2)}) async-start(), calls=%async_computation.3 | async-start | bytes 327680 | tf_op jit(solution)/shard_map/reduce_scatter | solution.py:57
  102.4 88.2 %all-reduce.6.cloned.1.call-start = ((), (), s32[]{:S(2)}) async-start(), calls=%async_computation.4 | async-start | bytes 524288 | tf_op jit(solution)/shard_map/psum | solution.py:40
  124.7 65.8 %copy-start.1 = (f32[512,128]{1,0:T(8,128)S(1)}, f32[512,128]{1,0:T(8,128)}, u32[]{:S(2)}) copy-start(f32[512,128]{1,0:T(8,128)} %all-reduce.4.cloned.1.call-done) | copy-start | bytes 786436
  135.4 98.6 %reduce-scatter.5.cloned.1.call-start = ((), (), s32[]{:S(2)}) async-start(), calls=%async_computation.5 | async-start | bytes 327680 | tf_op jit(solution)/shard_map/reduce_scatter | solution.py:57
  211.6 89.0 %all-reduce.8.cloned.1.call-start = ((), (), s32[]{:S(2)}) async-start(), calls=%async_computation.6 | async-start | bytes 524288 | tf_op jit(solution)/shard_map/psum | solution.py:40
  244.2 68.7 %copy-start.3 = (bf16[32,1024]{1,0:T(8,128)(2,1)S(1)}, bf16[32,1024]{1,0:T(8,128)(2,1)}, u32[]{:S(2)}) copy-start(bf16[32,1024]{1,0:T(8,128)(2,1)} %reduce-scatter.3.cloned.1.call-done) | copy-start | bytes 196612
  244.2 68.7 %copy-start.4 = (bf16[32,1024]{1,0:T(8,128)(2,1)S(1)}, bf16[32,1024]{1,0:T(8,128)(2,1)}, u32[]{:S(2)}) copy-start(bf16[32,1024]{1,0:T(8,128)(2,1)} %reduce-scatter.5.cloned.1.call-done) | copy-start | bytes 196612
Sparse Core Ops, SparseCore 0:
  34.2 55.1 all-reduce.3
  102.5 21.2 reduce-scatter.2
  135.5 55.0 all-reduce.5
  211.7 22.1 reduce-scatter.4
  245.5 55.0 all-reduce.7
where the time goes:
time: 321 us; the launch traced here: 320 us
  blocking collectives  145 us (45%)
  waiting for transfers between devices  130 us (40%)
  between operations  13.9 us (4%)
  other arithmetic  12.8 us (4%)
  local copies, waits for them, and re-layouts  11.6 us (4%)
  matrix products  6.53 us (2%)
    psum x3, waiting for transfers between devices, forward(): return lax.psum(partial_data, 'cell') * scale  86.5 us
    psum x2, blocking collectives, shards(): numer = lax.psum(placed, ('src', 'cell'))  78.6 us
    reduce_scatter x2, waiting for transfers between devices, shards(): lax.psum_scatter(partial_grad.astype(jnp.bfloat16), 'src', scatter_dimens...  43.7 us
    psum x4, blocking collectives, pair_total(): return lax.psum(values, 'src')  37.5 us
    all_gather x2, blocking collectives, shards(): lax.all_gather(grad_own.astype(jnp.bfloat16), 'src', axis=0, tiled=True)  18.7 us
    all_gather x1, blocking collectives, shards(): receivers = lax.all_gather(green_receiver, 'src', axis=0, tiled=True)  10.1 us
  transfers between devices with their start and end apart: 5, of which 5 were waited for; matrix products, arithmetic and copies ran while one was open for 0% of the time, Pallas kernels for 0%

commit v1 on v0

v1 whole, which is shorter than its diff:
```python
import functools
import math

import jax
import jax.numpy as jnp
from jax import lax
from jax.experimental import pallas as pl
from jax.experimental.pallas import tpu as pltpu
from jax.sharding import PartitionSpec as P

HSTEPS = 2
MESH = pl.DeviceIdType.MESH
F32 = jnp.float32
BF16 = jnp.bfloat16
NT = (((1,), (1,)), ((), ()))


def each(count, body, start=0):
    if count - start <= 8:
        for i in range(start, count):
            body(i)
    else:

        def step(i, carry):
            body(i)
            return carry

        lax.fori_loop(start, count, step, 0)


def kernel_body(
    n_s, n_c,
    gs, gr, ps, pr, order, models, noise,
    rec_out, res_out,
    gs_all, gr_all, ps_all, pr_all, nz_send, nz_recv,
    oper, rs_send, rs_recv, ag, stat_send, stat_recv,
    fin_send, fin_recv, wlow, res, grads,
    in_send, in_recv, rs_ssem, rs_rsem, ag_ssem, ag_rsem, st_ssem, st_rsem, fin_ssem, fin_rsem,
):
    s = lax.axis_index("src")
    c = lax.axis_index("cell")
    group_pairs = ps.shape[1]
    cells = gs.shape[1]
    models_count = models.shape[0]
    own = models_count // n_s
    share = group_pairs // n_c
    chunk = share * n_s
    pairs_all = group_pairs * n_s
    s_dev = gs.shape[0]
    receivers = gr.shape[0] * n_s
    scale = 1.0 / math.sqrt(cells * n_c)

    def src_peer(j):
        return lax.rem(s + j, n_s)

    def src_from(j):
        return lax.rem(s + n_s - j, n_s)

    def cell_peer(j):
        return lax.rem(c + j, n_c)

    def cell_from(j):
        return lax.rem(c + n_c - j, n_c)

    def to_src(src_ref, dst_ref, ssem, rsem, peer):
        return pltpu.make_async_remote_copy(
            src_ref=src_ref, dst_ref=dst_ref, send_sem=ssem, recv_sem=rsem,
            device_id={"src": peer}, device_id_type=MESH,
        )

    def to_cell(src_ref, dst_ref, ssem, rsem, peer):
        return pltpu.make_async_remote_copy(
            src_ref=src_ref, dst_ref=dst_ref, send_sem=ssem, recv_sem=rsem,
            device_id={"cell": peer}, device_id_type=MESH,
        )

    barrier = pltpu.get_barrier_semaphore()
    each(n_s, lambda j: pl.semaphore_signal(
        barrier, inc=1, device_id={"src": src_peer(j)}, device_id_type=MESH), 1)
    each(n_c, lambda j: pl.semaphore_signal(
        barrier, inc=1, device_id={"cell": cell_peer(j)}, device_id_type=MESH), 1)

    nz = noise[pl.ds(pl.multiple_of(c * share, share), share), :].astype(F32)
    nz_send[...] = nz.T.reshape(n_s, own, share).astype(BF16)

    pl.semaphore_wait(barrier, n_s + n_c - 2)

    def in_copies(j, slot, peer):
        return [
            to_src(gs, gs_all.at[slot], in_send.at[0, j], in_recv.at[0, j], peer),
            to_src(gr, gr_all.at[slot], in_send.at[1, j], in_recv.at[1, j], peer),
            to_src(ps, ps_all.at[slot], in_send.at[2, j], in_recv.at[2, j], peer),
            to_src(pr, pr_all.at[slot], in_send.at[3, j], in_recv.at[3, j], peer),
            to_src(nz_send.at[peer], nz_recv.at[slot], in_send.at[4, j], in_recv.at[4, j], peer),
        ]

    def start_inputs(j):
        for copy in in_copies(j, s, src_peer(j)):
            copy.start()

    each(n_s, start_inputs, 1)
    gs_all[s] = gs[...]
    gr_all[s] = gr[...]
    ps_all[s] = ps[...]
    pr_all[s] = pr[...]
    nz_recv[s] = nz_send[s]

    rows = lax.broadcasted_iota(jnp.int32, (cells, cells), 0)
    select = jnp.where(rows == order[...], 1.0, 0.0).astype(BF16)

    def wait_inputs(j):
        for copy in in_copies(j, src_from(j), src_peer(j)):
            copy.wait_recv()

    each(n_s, wait_inputs, 1)

    sources = n_s * s_dev
    fields = jnp.concatenate(
        [
            gs_all[...].astype(F32).reshape(sources, cells),
            gr_all[...].astype(F32).reshape(receivers, cells),
        ],
        axis=0,
    ).astype(BF16)
    placed = jnp.dot(fields, select, preferred_element_type=F32)
    source_cols = placed[:sources].astype(BF16)
    receiver_cols = placed[sources:].astype(BF16)

    def build(k):
        source_rows = lax.broadcasted_iota(jnp.int32, (sources, group_pairs), 0)
        receiver_rows = lax.broadcasted_iota(jnp.int32, (receivers, group_pairs), 0)
        pick_s = jnp.where(source_rows == ps_all[k] + k * s_dev, 1.0, 0.0).T.astype(BF16)
        pick_r = jnp.where(receiver_rows == pr_all[k], 1.0, 0.0).T.astype(BF16)
        block = (
            jnp.dot(pick_s, source_cols, preferred_element_type=F32)
            * jnp.dot(pick_r, receiver_cols, preferred_element_type=F32)
        ).astype(BF16)
        for t in range(n_c):
            at = pl.multiple_of(t * chunk + k * share, share)
            oper[pl.ds(at, share), :] = block[t * share : (t + 1) * share]

    def build_step(k, carry):
        build(k)
        return carry

    lax.fori_loop(0, n_s, build_step, 0)

    def rs_copy(phase, j, target):
        return to_cell(
            rs_send.at[phase, target], rs_recv.at[phase, j],
            rs_ssem.at[phase, j], rs_rsem.at[phase, j], target,
        )

    def forward(phase, low):
        def part(k):
            at = pl.multiple_of(k * chunk, chunk)
            return lax.dot_general(low, oper[pl.ds(at, chunk), :], NT, preferred_element_type=F32)

        def one(j):
            target = cell_peer(j)
            rs_send[phase, target] = part(target).astype(BF16)
            rs_copy(phase, j, target).start()

        each(n_c, one, 1)
        rs_total = part(c)
        each(n_c, lambda j: rs_copy(phase, j, cell_peer(j)).wait_recv(), 1)
        for j in range(1, n_c):
            rs_total = rs_total + rs_recv[phase, j].astype(F32)
        return rs_total * scale

    def ag_copy(phase, j, slot):
        return to_cell(
            ag.at[phase, slot], ag.at[phase, slot],
            ag_ssem.at[phase, j], ag_rsem.at[phase, j], cell_peer(j),
        )

    def gather(phase, value):
        ag[phase, c] = value.astype(BF16)
        each(n_c, lambda j: ag_copy(phase, j, c).start(), 1)
        each(n_c, lambda j: ag_copy(phase, j, cell_from(j)).wait_recv(), 1)
        return ag[phase].astype(F32)

    def stat_copy(step, j):
        return to_cell(
            stat_send.at[step], stat_recv.at[step, j],
            st_ssem.at[step, j], st_rsem.at[step, j], cell_peer(j),
        )

    def stat_start(step, columns):
        stacked = jnp.concatenate(
            [jnp.broadcast_to(column, (own, 128 // len(columns))) for column in columns], axis=1
        )
        stat_send[step] = stacked
        each(n_c, lambda j: stat_copy(step, j).start(), 1)

    def stat_total(step):
        each(n_c, lambda j: stat_copy(step, j).wait_recv(), 1)
        total = stat_send[step]
        for j in range(1, n_c):
            total = total + stat_recv[step, j]
        return total

    own_models = models[pl.ds(pl.multiple_of(s * own, own), own), :]
    own_noise = jnp.concatenate([nz_recv[k].astype(F32) for k in range(n_s)], axis=1)
    chunk_res = -(forward(0, own_models) + own_noise)
    res[...] = gather(0, chunk_res)

    def pair_sum(values):
        return jnp.sum(jnp.sum(values, axis=0), axis=1, keepdims=True)

    for step in range(HSTEPS):
        last = step == HSTEPS - 1
        full = res[...]
        spread = pair_sum(full * full)
        delta = jnp.sqrt(spread / pairs_all + 1e-06)
        weight = delta[None] / jnp.maximum(jnp.abs(full), delta[None])
        weighted = weight * full
        for k in range(n_c):
            wlow[:, k * chunk : (k + 1) * chunk] = weighted[k].astype(BF16)
        grad = jnp.dot(wlow[...], oper[...], preferred_element_type=F32) * scale
        grads[step] = grad
        numer_own = jnp.sum(grad * grad, axis=1, keepdims=True)
        if not last:
            stat_start(step, [numer_own])
        image = forward(step + 1, grad.astype(BF16))
        if last:
            own_full = chunk_res
            own_weight = delta / jnp.maximum(jnp.abs(own_full), delta)
            curve_own = jnp.sum(own_weight * image * image, axis=1, keepdims=True)
            stat_start(step, [numer_own, curve_own])
            total = stat_total(step)
            numer = total[:, 0:1]
            curvature = total[:, 64:65]
            alpha = numer / (curvature + 1e-06)
        else:
            images = gather(step + 1, image)
            numer = stat_total(step)[:, 0:1]
            curvature = pair_sum(weight * images * images)
            alpha = numer / (curvature + 1e-06)
            res[...] = full - alpha[None] * images
            grads[step] = alpha * grads[step]
        chunk_res = chunk_res - alpha * image

    for k in range(n_s):
        fin_send[k] = chunk_res[:, k * share : (k + 1) * share]

    def fin_copy(j, slot):
        return to_src(
            fin_send.at[src_peer(j)], fin_recv.at[slot], fin_ssem.at[j], fin_rsem.at[j], src_peer(j)
        )

    each(n_s, lambda j: fin_copy(j, s).start(), 1)
    fin_recv[s] = fin_send[s]
    total_rec = -(alpha * grads[HSTEPS - 1])
    for step in range(HSTEPS - 1):
        total_rec = total_rec - grads[step]
    rec_out[...] = total_rec

    def in_done(j):
        for copy in in_copies(j, s, src_peer(j)):
            copy.wait_send()

    each(n_s, in_done, 1)
    for phase in range(HSTEPS + 1):
        each(n_c, lambda j, phase=phase: rs_copy(phase, j, cell_peer(j)).wait_send(), 1)
    for phase in range(HSTEPS):
        each(n_c, lambda j, phase=phase: ag_copy(phase, j, c).wait_send(), 1)
        each(n_c, lambda j, phase=phase: stat_copy(phase, j).wait_send(), 1)
    each(n_s, lambda j: fin_copy(j, src_from(j)).wait_recv(), 1)
    res_out[...] = fin_recv[...].reshape(models_count, share).T
    each(n_s, lambda j: fin_copy(j, s).wait_send(), 1)


def shards(
    green_source, green_receiver, pair_source, pair_receiver, cell_order, test_models, data_noise
):
    n_s = lax.axis_size("src")
    n_c = lax.axis_size("cell")
    s_dev, cells = green_source.shape
    r_dev = green_receiver.shape[0]
    group_pairs = pair_source.shape[0]
    models_count = test_models.shape[0]
    own = models_count // n_s
    share = group_pairs // n_c
    chunk = share * n_s
    pairs_all = group_pairs * n_s
    dma = pltpu.SemaphoreType.DMA
    return pl.pallas_call(
        functools.partial(kernel_body, n_s, n_c),
        out_shape=(
            jax.ShapeDtypeStruct((own, cells), F32),
            jax.ShapeDtypeStruct((share, models_count), F32),
        ),
        in_specs=[pl.BlockSpec(memory_space=pltpu.VMEM)] * 7,
        out_specs=[pl.BlockSpec(memory_space=pltpu.VMEM)] * 2,
        scratch_shapes=[
            pltpu.VMEM((n_s, s_dev, cells), BF16),
            pltpu.VMEM((n_s, r_dev, cells), BF16),
            pltpu.VMEM((n_s, 1, group_pairs), jnp.int32),
            pltpu.VMEM((n_s, 1, group_pairs), jnp.int32),
            pltpu.VMEM((n_s, own, share), BF16),
            pltpu.VMEM((n_s, own, share), BF16),
            pltpu.VMEM((pairs_all, cells), BF16),
            pltpu.VMEM((HSTEPS + 1, n_c, own, chunk), BF16),
            pltpu.VMEM((HSTEPS + 1, n_c, own, chunk), BF16),
            pltpu.VMEM((HSTEPS, n_c, own, chunk), BF16),
            pltpu.VMEM((HSTEPS, own, 128), F32),
            pltpu.VMEM((HSTEPS, n_c, own, 128), F32),
            pltpu.VMEM((n_s, own, share), F32),
            pltpu.VMEM((n_s, own, share), F32),
            pltpu.VMEM((own, pairs_all), BF16),
            pltpu.VMEM((n_c, own, chunk), F32),
            pltpu.VMEM((HSTEPS, own, cells), F32),
            dma((5, n_s)), dma((5, n_s)),
            dma((HSTEPS + 1, n_c)), dma((HSTEPS + 1, n_c)),
            dma((HSTEPS, n_c)), dma((HSTEPS, n_c)),
            dma((HSTEPS, n_c)), dma((HSTEPS, n_c)),
            dma((n_s,)), dma((n_s,)),
        ],
        compiler_params=pltpu.CompilerParams(
            collective_id=0, has_side_effects=True, vmem_limit_bytes=56 * 1024 * 1024
        ),
    )(
        green_source, green_receiver, pair_source[None, :], pair_receiver[None, :],
        cell_order, test_models, data_noise,
    )


def solution(mesh):
    return jax.shard_map(
        shards,
        mesh=mesh,
        in_specs=(
            P("src", "cell"),
            P("src", "cell"),
            P("src"),
            P("src"),
            P("cell", None),
            P(None, "cell"),
            P("src", None),
        ),
        out_specs=(P("src", "cell"), P(("src", "cell"), None)),
        check_vma=False,
    )
```

time: 321 us -> 58.7 us (0.18)
  blocking collectives: 145 us -> 0 us
  waiting for transfers between devices: 130 us -> 0 us
  Pallas kernels: 0 us -> 55.7 us
  between operations: 13.9 us -> 0.65 us
  other arithmetic: 12.8 us -> 0 us
  local copies, waits for them, and re-layouts: 11.6 us -> 2.19 us
  matrix products: 6.53 us -> 0 us
    psum x6 -> x0, blocking collectives: 116 us -> none  [the longest x2 78.6 us: shards(): numer = lax.psum(placed, ('src', 'cell'))]
    psum x3 -> x0, waiting for transfers between devices: 86.5 us -> none  [forward(): return lax.psum(partial_data, 'cell') * scale]
    pallas_call x0 -> x1, Pallas kernels: none -> 55.7 us  [shards(): pl.pallas_call(functools.partial(kernel_body, n_s, n_c), out_shape=(jax.S...]
    reduce_scatter x2 -> x0, waiting for transfers between devices: 43.7 us -> none  [shards(): lax.psum_scatter(partial_grad.astype(jnp.bfloat16), 'src', scatter_dimens...]
    all_gather x3 -> x0, blocking collectives: 28.8 us -> none  [the longest x2 18.7 us: shards(): lax.all_gather(grad_own.astype(jnp.bfloat16), 'src', axis=0, tiled=True)]
    gather x4 -> x0, local copies, waits for them, and re-layouts: 10.5 us -> none  [the longest x1 3.21 us: shards(): source_cols = jnp.take(green_source, order, axis=1)]
    dot_general x5 -> x0, matrix products: 6.53 us -> none  [the longest x3 3.46 us: forward(): lax.dot_general(kernel, models_low, contract_cells, preferred_element_typ...]
    reduce_sum x5 -> x0, other arithmetic: 5.16 us -> none  [the longest x2 2.12 us: shards(): totals = pair_total(jnp.sum(weight * image * image, axis=0)[None, :])]
  transfers between devices with their start and end apart: 5 -> 0, of which waited for: 5 -> 0; matrix products, arithmetic and copies ran while one was open for 0% -> 0% of each run, Pallas kernels for 0% -> 0%
where the time goes in v1:
time: 58.7 us; the launch traced here: 58.5 us
  Pallas kernels  55.7 us (95%)
  local copies, waits for them, and re-layouts  2.19 us (4%)
  between operations  0.65 us (1%)
    pallas_call x1, Pallas kernels, shards(): pl.pallas_call(functools.partial(kernel_body, n_s, n_c), out_shape=(jax.S...  55.7 us
    unnamed x4, local copies, waits for them, and re-layouts  2.19 us

profile of v1, /device:TPU:0, one launch (start us, length us, event | category | flops | bytes accessed | tf_op | source)
XLA Modules:
  0.0 58.5 jit_solution(10458510219906168541)
XLA Ops:
  0.6 55.7 %shard_map.86 = (f32[32,1024]{1,0:T(8,128)}, f32[64,128]{1,0:T(8,128)}) custom-call(bf16[8,1024]{1,0:T(8,128)(2,1)} %gs.1, bf16[16,1024]{1,0:T(8,128)(2,1)} %gr.1, s32[1,512]{1,0:T(1,128)} %bitcast.2, s32[1,512]{1,0:T(1,128)} %bitcast.3, s32[1,1024]{1,0:T(1,128)} %order.1, bf16[128,1024]{1,0:T(8,128)(2,1)} %models.1, bf16[512,128]{1,0:T(8,128)(2,1)} %noise.1), custom_call_target="tpu_custom_call" | custom-call | tf_op jit(solution)/shard_map/pallas_call | solution.py:288
  56.3 0.0 copy-start
  56.3 1.6 %copy.11 = f32[32,1024]{1,0:T(8,128)} copy(f32[32,1024]{1,0:T(8,128)} %get-tuple-element.4) | data formatting | bytes 262144
  57.9 0.0 copy-done
  57.9 0.6 %copy.12 = f32[64,128]{1,0:T(8,128)} copy(f32[64,128]{1,0:T(8,128)S(1)} %copy-done) | data formatting | bytes 65536
Async XLA Ops:
  56.3 1.6 %copy-start = (f32[64,128]{1,0:T(8,128)S(1)}, f32[64,128]{1,0:T(8,128)}, u32[]{:S(2)}) copy-start(f32[64,128]{1,0:T(8,128)} %get-tuple-element.5) | copy-start | bytes 98308

commit v2 on v1

v2 whole, which is shorter than its diff:
```python
import functools
import math

import jax
import jax.numpy as jnp
from jax import lax
from jax.experimental import pallas as pl
from jax.experimental.pallas import tpu as pltpu
from jax.sharding import PartitionSpec as P

HSTEPS = 2
MESH = pl.DeviceIdType.MESH
F32 = jnp.float32
BF16 = jnp.bfloat16
NT = (((1,), (1,)), ((), ()))


def each(count, body):
    if count <= 8:
        for i in range(count - 1, 0, -1):
            body(i)
    else:

        def step(i, carry):
            body(count - i)
            return carry

        lax.fori_loop(1, count, step, 0)


def kernel_body(
    n_s, n_c,
    gs, gr, ps, pr, order, models, noise,
    rec_out, res_out,
    gs_in, gr_in, order_in, models_in, noise_in,
    fields, indices, nz_send, nz_recv,
    oper, rs_send, rs_recv, ag, stat_send, stat_recv,
    fin_send, fin_recv, wlow, res, grads,
    load, in_send, in_recv, rs_ssem, rs_rsem, ag_ssem, ag_rsem, st_ssem, st_rsem, fin_ssem, fin_rsem,
):
    s = lax.axis_index("src")
    c = lax.axis_index("cell")
    group_pairs = ps.shape[1]
    cells = gs.shape[1]
    models_count = models.shape[0]
    own = models_count // n_s
    share = group_pairs // n_c
    chunk = share * n_s
    pairs_all = group_pairs * n_s
    s_dev = gs.shape[0]
    receivers = gr.shape[0] * n_s
    scale = 1.0 / math.sqrt(cells * n_c)

    def src_peer(j):
        return jnp.bitwise_xor(s, j)

    def cell_peer(j):
        return jnp.bitwise_xor(c, j)

    def to_src(src_ref, dst_ref, ssem, rsem, peer):
        return pltpu.make_async_remote_copy(
            src_ref=src_ref, dst_ref=dst_ref, send_sem=ssem, recv_sem=rsem,
            device_id={"src": peer}, device_id_type=MESH,
        )

    def to_cell(src_ref, dst_ref, ssem, rsem, peer):
        return pltpu.make_async_remote_copy(
            src_ref=src_ref, dst_ref=dst_ref, send_sem=ssem, recv_sem=rsem,
            device_id={"cell": peer}, device_id_type=MESH,
        )

    barrier = pltpu.get_barrier_semaphore()
    each(n_s, lambda j: pl.semaphore_signal(
        barrier, inc=1, device_id={"src": src_peer(j)}, device_id_type=MESH))
    each(n_c, lambda j: pl.semaphore_signal(
        barrier, inc=1, device_id={"cell": cell_peer(j)}, device_id_type=MESH))

    loads = [
        pltpu.make_async_copy(order, order_in, load.at[0]),
        pltpu.make_async_copy(gs, gs_in, load.at[1]),
        pltpu.make_async_copy(gr, gr_in, load.at[2]),
        pltpu.make_async_copy(ps, indices.at[s, 0], load.at[3]),
        pltpu.make_async_copy(pr, indices.at[s, 1], load.at[4]),
        pltpu.make_async_copy(
            noise.at[pl.ds(pl.multiple_of(c * share, share), share), :], noise_in, load.at[5]),
        pltpu.make_async_copy(
            models.at[pl.ds(pl.multiple_of(s * own, own), own), :], models_in, load.at[6]),
    ]
    for copy in loads:
        copy.start()
    for copy in loads:
        copy.wait()
    rows = lax.broadcasted_iota(jnp.int32, (cells, cells), 0)
    select = jnp.where(rows == order_in[...], 1.0, 0.0).astype(BF16)
    raw = jnp.concatenate([gs_in[...].astype(F32), gr_in[...].astype(F32)], axis=0).astype(BF16)
    fields[s] = jnp.dot(raw, select, preferred_element_type=F32).astype(BF16)
    nz_send[...] = noise_in[...].astype(F32).T.reshape(n_s, own, share).astype(BF16)
    nz_recv[s] = nz_send[s]

    pl.semaphore_wait(barrier, n_s + n_c - 2)

    def in_copies(j, slot):
        peer = src_peer(j)
        return [
            to_src(fields.at[slot], fields.at[slot], in_send.at[0, j], in_recv.at[0, j], peer),
            to_src(indices.at[slot], indices.at[slot], in_send.at[1, j], in_recv.at[1, j], peer),
            to_src(nz_send.at[peer], nz_recv.at[slot], in_send.at[2, j], in_recv.at[2, j], peer),
        ]

    def start_inputs(j):
        for copy in in_copies(j, s):
            copy.start()

    each(n_s, start_inputs)

    def wait_inputs(j):
        for copy in in_copies(j, src_peer(j)):
            copy.wait_recv()

    each(n_s, wait_inputs)

    sources = n_s * s_dev
    every = fields[...].astype(F32)
    source_cols = every[:, :s_dev].reshape(sources, cells).astype(BF16)
    receiver_cols = every[:, s_dev:].reshape(receivers, cells).astype(BF16)

    def build(k):
        source_rows = lax.broadcasted_iota(jnp.int32, (sources, group_pairs), 0)
        receiver_rows = lax.broadcasted_iota(jnp.int32, (receivers, group_pairs), 0)
        pick_s = jnp.where(source_rows == indices[k, 0] + k * s_dev, 1.0, 0.0).T.astype(BF16)
        pick_r = jnp.where(receiver_rows == indices[k, 1], 1.0, 0.0).T.astype(BF16)
        block = (
            jnp.dot(pick_s, source_cols, preferred_element_type=F32)
            * jnp.dot(pick_r, receiver_cols, preferred_element_type=F32)
        ).astype(BF16)
        for t in range(n_c):
            at = pl.multiple_of(t * chunk + k * share, share)
            oper[pl.ds(at, share), :] = block[t * share : (t + 1) * share]

    def build_step(k, carry):
        build(k)
        return carry

    lax.fori_loop(0, n_s, build_step, 0)

    def rs_copy(phase, j, target):
        return to_cell(
            rs_send.at[phase, target], rs_recv.at[phase, j],
            rs_ssem.at[phase, j], rs_rsem.at[phase, j], target,
        )

    def forward(phase, low):
        def part(k):
            at = pl.multiple_of(k * chunk, chunk)
            return lax.dot_general(low, oper[pl.ds(at, chunk), :], NT, preferred_element_type=F32)

        def one(j):
            target = cell_peer(j)
            rs_send[phase, target] = part(target).astype(BF16)
            rs_copy(phase, j, target).start()

        each(n_c, one)
        rs_total = part(c)
        each(n_c, lambda j: rs_copy(phase, j, cell_peer(j)).wait_recv())
        for j in range(1, n_c):
            rs_total = rs_total + rs_recv[phase, j].astype(F32)
        return rs_total * scale

    def ag_copy(phase, j, slot):
        return to_cell(
            ag.at[phase, slot], ag.at[phase, slot],
            ag_ssem.at[phase, j], ag_rsem.at[phase, j], cell_peer(j),
        )

    def gather(phase, value):
        ag[phase, c] = value.astype(BF16)
        each(n_c, lambda j: ag_copy(phase, j, c).start())
        each(n_c, lambda j: ag_copy(phase, j, cell_peer(j)).wait_recv())
        return ag[phase].astype(F32)

    def stat_copy(step, j):
        return to_cell(
            stat_send.at[step], stat_recv.at[step, j],
            st_ssem.at[step, j], st_rsem.at[step, j], cell_peer(j),
        )

    diagonal = lax.broadcasted_iota(jnp.int32, (own, own), 0) == lax.broadcasted_iota(
        jnp.int32, (own, own), 1
    )

    def to_row(column):
        return jnp.sum(jnp.where(diagonal, column, 0.0), axis=0, keepdims=True)

    def to_column(row):
        return jnp.sum(jnp.where(diagonal, row, 0.0), axis=1, keepdims=True)

    def stat_start(step, first, second):
        top = lax.broadcasted_iota(jnp.int32, (8, own), 0) == 0
        stat_send[step] = jnp.where(top, to_row(first), to_row(second))
        each(n_c, lambda j: stat_copy(step, j).start())

    def stat_total(step):
        each(n_c, lambda j: stat_copy(step, j).wait_recv())
        total = stat_send[step]
        for j in range(1, n_c):
            total = total + stat_recv[step, j]
        return to_column(total[0:1]), to_column(total[1:2])

    own_models = models_in[...]
    own_noise = jnp.concatenate([nz_recv[k].astype(F32) for k in range(n_s)], axis=1)
    chunk_res = -(forward(0, own_models) + own_noise)
    res[...] = gather(0, chunk_res)

    def pair_sum(values):
        return jnp.sum(jnp.sum(values, axis=0), axis=1, keepdims=True)

    for step in range(HSTEPS):
        last = step == HSTEPS - 1
        full = res[...]
        spread = pair_sum(full * full)
        delta = jnp.sqrt(spread / pairs_all + 1e-06)
        weight = delta[None] / jnp.maximum(jnp.abs(full), delta[None])
        weighted = weight * full
        for k in range(n_c):
            wlow[:, k * chunk : (k + 1) * chunk] = weighted[k].astype(BF16)
        grad = jnp.dot(wlow[...], oper[...], preferred_element_type=F32) * scale
        grads[step] = grad
        numer_own = jnp.sum(grad * grad, axis=1, keepdims=True)
        if not last:
            stat_start(step, numer_own, numer_own)
        image = forward(step + 1, grad.astype(BF16))
        if last:
            own_full = chunk_res
            own_weight = delta / jnp.maximum(jnp.abs(own_full), delta)
            curve_own = jnp.sum(own_weight * image * image, axis=1, keepdims=True)
            stat_start(step, numer_own, curve_own)
            numer, curvature = stat_total(step)
            alpha = numer / (curvature + 1e-06)
        else:
            images = gather(step + 1, image)
            numer, _ = stat_total(step)
            curvature = pair_sum(weight * images * images)
            alpha = numer / (curvature + 1e-06)
            res[...] = full - alpha[None] * images
            grads[step] = alpha * grads[step]
        chunk_res = chunk_res - alpha * image

    for k in range(n_s):
        fin_send[k] = chunk_res[:, k * share : (k + 1) * share]

    def fin_copy(j, slot):
        return to_src(
            fin_send.at[src_peer(j)], fin_recv.at[slot], fin_ssem.at[j], fin_rsem.at[j], src_peer(j)
        )

    each(n_s, lambda j: fin_copy(j, s).start())
    fin_recv[s] = fin_send[s]
    total_rec = -(alpha * grads[HSTEPS - 1])
    for step in range(HSTEPS - 1):
        total_rec = total_rec - grads[step]
    rec_out[...] = total_rec

    def in_done(j):
        for copy in in_copies(j, s):
            copy.wait_send()

    each(n_s, in_done)
    for phase in range(HSTEPS + 1):
        each(n_c, lambda j, phase=phase: rs_copy(phase, j, cell_peer(j)).wait_send())
    for phase in range(HSTEPS):
        each(n_c, lambda j, phase=phase: ag_copy(phase, j, c).wait_send())
        each(n_c, lambda j, phase=phase: stat_copy(phase, j).wait_send())
    each(n_s, lambda j: fin_copy(j, src_peer(j)).wait_recv())
    res_out[...] = fin_recv[...].reshape(models_count, share).T
    each(n_s, lambda j: fin_copy(j, s).wait_send())


def shards(
    green_source, green_receiver, pair_source, pair_receiver, cell_order, test_models, data_noise
):
    n_s = lax.axis_size("src")
    n_c = lax.axis_size("cell")
    s_dev, cells = green_source.shape
    r_dev = green_receiver.shape[0]
    group_pairs = pair_source.shape[0]
    models_count = test_models.shape[0]
    own = models_count // n_s
    share = group_pairs // n_c
    chunk = share * n_s
    pairs_all = group_pairs * n_s
    dma = pltpu.SemaphoreType.DMA
    return pl.pallas_call(
        functools.partial(kernel_body, n_s, n_c),
        out_shape=(
            pltpu.VMEM((own, cells), F32),
            pltpu.VMEM((share, models_count), F32),
        ),
        in_specs=[pl.BlockSpec(memory_space=pltpu.HBM)] * 7,
        out_specs=[pl.BlockSpec(memory_space=pltpu.VMEM)] * 2,
        scratch_shapes=[
            pltpu.VMEM((s_dev, cells), BF16),
            pltpu.VMEM((r_dev, cells), BF16),
            pltpu.VMEM((1, cells), jnp.int32),
            pltpu.VMEM((own, cells), BF16),
            pltpu.VMEM((share, models_count), BF16),
            pltpu.VMEM((n_s, s_dev + r_dev, cells), BF16),
            pltpu.VMEM((n_s, 2, 1, group_pairs), jnp.int32),
            pltpu.VMEM((n_s, own, share), BF16),
            pltpu.VMEM((n_s, own, share), BF16),
            pltpu.VMEM((pairs_all, cells), BF16),
            pltpu.VMEM((HSTEPS + 1, n_c, own, chunk), BF16),
            pltpu.VMEM((HSTEPS + 1, n_c, own, chunk), BF16),
            pltpu.VMEM((HSTEPS, n_c, own, chunk), BF16),
            pltpu.VMEM((HSTEPS, 8, own), F32),
            pltpu.VMEM((HSTEPS, n_c, 8, own), F32),
            pltpu.VMEM((n_s, own, share), F32),
            pltpu.VMEM((n_s, own, share), F32),
            pltpu.VMEM((own, pairs_all), BF16),
            pltpu.VMEM((n_c, own, chunk), F32),
            pltpu.VMEM((HSTEPS, own, cells), F32),
            dma((7,)), dma((3, n_s)), dma((3, n_s)),
            dma((HSTEPS + 1, n_c)), dma((HSTEPS + 1, n_c)),
            dma((HSTEPS, n_c)), dma((HSTEPS, n_c)),
            dma((HSTEPS, n_c)), dma((HSTEPS, n_c)),
            dma((n_s,)), dma((n_s,)),
        ],
        compiler_params=pltpu.CompilerParams(
            collective_id=0, has_side_effects=True, vmem_limit_bytes=60 * 1024 * 1024
        ),
    )(
        green_source, green_receiver, pair_source[None, :], pair_receiver[None, :],
        cell_order, test_models, data_noise,
    )


def solution(mesh):
    return jax.shard_map(
        shards,
        mesh=mesh,
        in_specs=(
            P("src", "cell"),
            P("src", "cell"),
            P("src"),
            P("src"),
            P("cell", None),
            P(None, "cell"),
            P("src", None),
        ),
        out_specs=(P("src", "cell"), P(("src", "cell"), None)),
        check_vma=False,
    )
```

time: 58.7 us -> 51.6 us (0.88)
  Pallas kernels: 55.7 us -> 49.5 us
  local copies, waits for them, and re-layouts: 2.19 us -> 1.27 us
    pallas_call x1, Pallas kernels: 55.7 us -> 49.5 us  [shards(): pl.pallas_call(functools.partial(kernel_body, n_s, n_c), out_shape=(pltpu...]
    unnamed x4 -> x2, local copies, waits for them, and re-layouts: 2.19 us -> 1.27 us
where the time goes in v2:
time: 51.6 us; the launch traced here: 51.4 us
  Pallas kernels  49.5 us (96%)
  local copies, waits for them, and re-layouts  1.27 us (2%)
  between operations  0.64 us (1%)
    pallas_call x1, Pallas kernels, shards(): pl.pallas_call(functools.partial(kernel_body, n_s, n_c), out_shape=(pltpu...  49.5 us
    unnamed x2, local copies, waits for them, and re-layouts  1.27 us

profile of v2, /device:TPU:0, one launch (start us, length us, event | category | flops | bytes accessed | tf_op | source)
XLA Modules:
  0.0 51.4 jit_solution(7608412498176293749)
XLA Ops:
  0.6 49.5 %shard_map.86 = (f32[32,1024]{1,0:T(8,128)S(1)}, f32[64,128]{1,0:T(8,128)S(1)}) custom-call(bf16[8,1024]{1,0:T(8,128)(2,1)} %gs.1, bf16[16,1024]{1,0:T(8,128)(2,1)} %gr.1, s32[1,512]{1,0:T(1,128)} %bitcast.2, s32[1,512]{1,0:T(1,128)} %bitcast.3, s32[1,1024]{1,0:T(1,128)} %order.1, bf16[128,1024]{1,0:T(8,128)(2,1)} %models.1, bf16[512,128]{1,0:T(8,128)(2,1)} %noise.1), custom_call_target="tpu_custom_call" | custom-call | tf_op jit(solution)/shard_map/pallas_call | solution.py:292
  50.2 0.7 %copy.11 = f32[32,1024]{1,0:T(8,128)} copy(f32[32,1024]{1,0:T(8,128)S(1)} %get-tuple-element.2) | data formatting | bytes 262144
  50.8 0.6 %copy.12 = f32[64,128]{1,0:T(8,128)} copy(f32[64,128]{1,0:T(8,128)S(1)} %get-tuple-element.3) | data formatting | bytes 65536

commit v3 on v2

--- a/solution.py
+++ b/solution.py
@@ -34,7 +34,7 @@
     rec_out, res_out,
     gs_in, gr_in, order_in, models_in, noise_in,
     fields, indices, nz_send, nz_recv,
-    oper, rs_send, rs_recv, ag, stat_send, stat_recv,
+    picks, oper, rs_send, rs_recv, ag, stat_send, stat_recv,
     fin_send, fin_recv, wlow, res, grads,
     load, in_send, in_recv, rs_ssem, rs_rsem, ag_ssem, ag_rsem, st_ssem, st_rsem, fin_ssem, fin_rsem,
 ):
@@ -48,7 +48,7 @@
     chunk = share * n_s
     pairs_all = group_pairs * n_s
     s_dev = gs.shape[0]
-    receivers = gr.shape[0] * n_s
+    r_dev = gr.shape[0]
     scale = 1.0 / math.sqrt(cells * n_c)
 
     def src_peer(j):
@@ -99,13 +99,14 @@
 
     pl.semaphore_wait(barrier, n_s + n_c - 2)
 
-    def in_copies(j, slot):
+    def in_copies(j, slot, which=(0, 1, 2)):
         peer = src_peer(j)
-        return [
-            to_src(fields.at[slot], fields.at[slot], in_send.at[0, j], in_recv.at[0, j], peer),
-            to_src(indices.at[slot], indices.at[slot], in_send.at[1, j], in_recv.at[1, j], peer),
-            to_src(nz_send.at[peer], nz_recv.at[slot], in_send.at[2, j], in_recv.at[2, j], peer),
+        makers = [
+            lambda: to_src(fields.at[slot], fields.at[slot], in_send.at[0, j], in_recv.at[0, j], peer),
+            lambda: to_src(indices.at[slot], indices.at[slot], in_send.at[1, j], in_recv.at[1, j], peer),
+            lambda: to_src(nz_send.at[peer], nz_recv.at[slot], in_send.at[2, j], in_recv.at[2, j], peer),
         ]
+        return [makers[n]() for n in which]
 
     def start_inputs(j):
         for copy in in_copies(j, s):
@@ -113,35 +114,42 @@
 
     each(n_s, start_inputs)
 
+    dev_rows = s_dev + r_dev
+    field_rows = n_s * dev_rows
+    row = lax.broadcasted_iota(jnp.int32, (field_rows, 1), 0)
+    group = jnp.zeros((field_rows, 1), jnp.int32)
+    for k in range(1, n_s):
+        group = group + jnp.where(row >= k * dev_rows, 1, 0)
+    within = row - group * dev_rows
+    is_source = within < s_dev
+    source_id = jnp.where(is_source, group * s_dev + within, -1)
+    receiver_id = jnp.where(is_source, -1, group * r_dev + within - s_dev)
+
     def wait_inputs(j):
-        for copy in in_copies(j, src_peer(j)):
+        for copy in in_copies(j, src_peer(j), (0, 1)):
             copy.wait_recv()
 
     each(n_s, wait_inputs)
 
-    sources = n_s * s_dev
-    every = fields[...].astype(F32)
-    source_cols = every[:, :s_dev].reshape(sources, cells).astype(BF16)
-    receiver_cols = every[:, s_dev:].reshape(receivers, cells).astype(BF16)
+    for k in range(n_s):
+        hit = (source_id == indices[k, 0] + k * s_dev) | (receiver_id == indices[k, 1])
+        pick = jnp.where(hit, 1.0, 0.0).T.astype(BF16)
+        for t in range(n_c):
+            at = t * chunk + k * share
+            picks[at : at + share, :] = pick[t * share : (t + 1) * share]
+    every = fields[...].astype(F32).reshape(field_rows, cells)
+    source_cols = jnp.where(is_source, every, 0.0).astype(BF16)
+    receiver_cols = jnp.where(is_source, 0.0, every).astype(BF16)
 
     def build(k):
-        source_rows = lax.broadcasted_iota(jnp.int32, (sources, group_pairs), 0)
-        receiver_rows = lax.broadcasted_iota(jnp.int32, (receivers, group_pairs), 0)
-        pick_s = jnp.where(source_rows == indices[k, 0] + k * s_dev, 1.0, 0.0).T.astype(BF16)
-        pick_r = jnp.where(receiver_rows == indices[k, 1], 1.0, 0.0).T.astype(BF16)
+        at = pl.multiple_of(k * chunk, chunk)
+        pick = picks[pl.ds(at, chunk), :]
         block = (
-            jnp.dot(pick_s, source_cols, preferred_element_type=F32)
-            * jnp.dot(pick_r, receiver_cols, preferred_element_type=F32)
+            jnp.dot(pick, source_cols, preferred_element_type=F32)
+            * jnp.dot(pick, receiver_cols, preferred_element_type=F32)
         ).astype(BF16)
-        for t in range(n_c):
-            at = pl.multiple_of(t * chunk + k * share, share)
-            oper[pl.ds(at, share), :] = block[t * share : (t + 1) * share]
-
-    def build_step(k, carry):
-        build(k)
-        return carry
-
-    lax.fori_loop(0, n_s, build_step, 0)
+        oper[pl.ds(at, chunk), :] = block
+        return block
 
     def rs_copy(phase, j, target):
         return to_cell(
@@ -149,10 +157,11 @@
             rs_ssem.at[phase, j], rs_rsem.at[phase, j], target,
         )
 
-    def forward(phase, low):
+    def forward(phase, low, after_sends):
         def part(k):
             at = pl.multiple_of(k * chunk, chunk)
-            return lax.dot_general(low, oper[pl.ds(at, chunk), :], NT, preferred_element_type=F32)
+            block = build(k) if phase == 0 else oper[pl.ds(at, chunk), :]
+            return lax.dot_general(low, block, NT, preferred_element_type=F32)
 
         def one(j):
             target = cell_peer(j)
@@ -160,6 +169,7 @@
             rs_copy(phase, j, target).start()
 
         each(n_c, one)
+        after_sends()
         rs_total = part(c)
         each(n_c, lambda j: rs_copy(phase, j, cell_peer(j)).wait_recv())
         for j in range(1, n_c):
@@ -207,8 +217,10 @@
         return to_column(total[0:1]), to_column(total[1:2])
 
     own_models = models_in[...]
+    first_data = forward(0, own_models, lambda: None)
+    each(n_s, lambda j: in_copies(j, src_peer(j), (2,))[0].wait_recv())
     own_noise = jnp.concatenate([nz_recv[k].astype(F32) for k in range(n_s)], axis=1)
-    chunk_res = -(forward(0, own_models) + own_noise)
+    chunk_res = -(first_data + own_noise)
     res[...] = gather(0, chunk_res)
 
     def pair_sum(values):
@@ -226,9 +238,12 @@
         grad = jnp.dot(wlow[...], oper[...], preferred_element_type=F32) * scale
         grads[step] = grad
         numer_own = jnp.sum(grad * grad, axis=1, keepdims=True)
-        if not last:
-            stat_start(step, numer_own, numer_own)
-        image = forward(step + 1, grad.astype(BF16))
+
+        def send_numer():
+            if not last:
+                stat_start(step, numer_own, numer_own)
+
+        image = forward(step + 1, grad.astype(BF16), send_numer)
         if last:
             own_full = chunk_res
             own_weight = delta / jnp.maximum(jnp.abs(own_full), delta)
@@ -307,6 +322,7 @@
             pltpu.VMEM((n_s, 2, 1, group_pairs), jnp.int32),
             pltpu.VMEM((n_s, own, share), BF16),
             pltpu.VMEM((n_s, own, share), BF16),
+            pltpu.VMEM((pairs_all, n_s * (s_dev + r_dev)), BF16),
             pltpu.VMEM((pairs_all, cells), BF16),
             pltpu.VMEM((HSTEPS + 1, n_c, own, chunk), BF16),
             pltpu.VMEM((HSTEPS + 1, n_c, own, chunk), BF16),

time: 51.6 us -> 49.9 us (0.967)
  Pallas kernels: 49.5 us -> 47.8 us
    pallas_call x1, Pallas kernels: 49.5 us -> 47.8 us  [shards(): pl.pallas_call(functools.partial(kernel_body, n_s, n_c), out_shape=(pltpu...]
where the time goes in v3:
time: 49.9 us; the launch traced here: 49.7 us
  Pallas kernels  47.8 us (96%)
  local copies, waits for them, and re-layouts  1.27 us (3%)
  between operations  0.64 us (1%)
    pallas_call x1, Pallas kernels, shards(): pl.pallas_call(functools.partial(kernel_body, n_s, n_c), out_shape=(pltpu...  47.8 us
    unnamed x2, local copies, waits for them, and re-layouts  1.27 us

profile of v3, /device:TPU:0, one launch (start us, length us, event | category | flops | bytes accessed | tf_op | source)
XLA Modules:
  0.0 49.7 jit_solution(2344200162699272808)
XLA Ops:
  0.6 47.8 %shard_map.86 = (f32[32,1024]{1,0:T(8,128)S(1)}, f32[64,128]{1,0:T(8,128)S(1)}) custom-call(bf16[8,1024]{1,0:T(8,128)(2,1)} %gs.1, bf16[16,1024]{1,0:T(8,128)(2,1)} %gr.1, s32[1,512]{1,0:T(1,128)} %bitcast.2, s32[1,512]{1,0:T(1,128)} %bitcast.3, s32[1,1024]{1,0:T(1,128)} %order.1, bf16[128,1024]{1,0:T(8,128)(2,1)} %models.1, bf16[512,128]{1,0:T(8,128)(2,1)} %noise.1), custom_call_target="tpu_custom_call" | custom-call | tf_op jit(solution)/shard_map/pallas_call | solution.py:307
  48.4 0.7 %copy.11 = f32[32,1024]{1,0:T(8,128)} copy(f32[32,1024]{1,0:T(8,128)S(1)} %get-tuple-element.2) | data formatting | bytes 262144
  49.1 0.6 %copy.12 = f32[64,128]{1,0:T(8,128)} copy(f32[64,128]{1,0:T(8,128)S(1)} %get-tuple-element.3) | data formatting | bytes 65536

commit v4 on v3

--- a/solution.py
+++ b/solution.py
@@ -108,11 +108,9 @@
         ]
         return [makers[n]() for n in which]
 
-    def start_inputs(j):
-        for copy in in_copies(j, s):
-            copy.start()
-
-    each(n_s, start_inputs)
+    each(n_s, lambda j: in_copies(j, s, (1,))[0].start())
+    each(n_s, lambda j: in_copies(j, s, (0,))[0].start())
+    each(n_s, lambda j: in_copies(j, s, (2,))[0].start())
 
     dev_rows = s_dev + r_dev
     field_rows = n_s * dev_rows
@@ -125,11 +123,7 @@
     source_id = jnp.where(is_source, group * s_dev + within, -1)
     receiver_id = jnp.where(is_source, -1, group * r_dev + within - s_dev)
 
-    def wait_inputs(j):
-        for copy in in_copies(j, src_peer(j), (0, 1)):
-            copy.wait_recv()
-
-    each(n_s, wait_inputs)
+    each(n_s, lambda j: in_copies(j, src_peer(j), (1,))[0].wait_recv())
 
     for k in range(n_s):
         hit = (source_id == indices[k, 0] + k * s_dev) | (receiver_id == indices[k, 1])
@@ -137,6 +131,7 @@
         for t in range(n_c):
             at = t * chunk + k * share
             picks[at : at + share, :] = pick[t * share : (t + 1) * share]
+    each(n_s, lambda j: in_copies(j, src_peer(j), (0,))[0].wait_recv())
     every = fields[...].astype(F32).reshape(field_rows, cells)
     source_cols = jnp.where(is_source, every, 0.0).astype(BF16)
     receiver_cols = jnp.where(is_source, 0.0, every).astype(BF16)
@@ -226,6 +221,7 @@
     def pair_sum(values):
         return jnp.sum(jnp.sum(values, axis=0), axis=1, keepdims=True)
 
+    alphas = []
     for step in range(HSTEPS):
         last = step == HSTEPS - 1
         full = res[...]
@@ -236,19 +232,21 @@
         for k in range(n_c):
             wlow[:, k * chunk : (k + 1) * chunk] = weighted[k].astype(BF16)
         grad = jnp.dot(wlow[...], oper[...], preferred_element_type=F32) * scale
-        grads[step] = grad
-        numer_own = jnp.sum(grad * grad, axis=1, keepdims=True)
+        after = []
 
         def send_numer():
-            if not last:
+            grads[step] = grad
+            numer_own = jnp.sum(grad * grad, axis=1, keepdims=True)
+            after.append(numer_own)
+            if last:
+                after.append(delta / jnp.maximum(jnp.abs(chunk_res), delta))
+            else:
                 stat_start(step, numer_own, numer_own)
 
         image = forward(step + 1, grad.astype(BF16), send_numer)
         if last:
-            own_full = chunk_res
-            own_weight = delta / jnp.maximum(jnp.abs(own_full), delta)
-            curve_own = jnp.sum(own_weight * image * image, axis=1, keepdims=True)
-            stat_start(step, numer_own, curve_own)
+            curve_own = jnp.sum(after[1] * image * image, axis=1, keepdims=True)
+            stat_start(step, after[0], curve_own)
             numer, curvature = stat_total(step)
             alpha = numer / (curvature + 1e-06)
         else:
@@ -257,8 +255,8 @@
             curvature = pair_sum(weight * images * images)
             alpha = numer / (curvature + 1e-06)
             res[...] = full - alpha[None] * images
-            grads[step] = alpha * grads[step]
         chunk_res = chunk_res - alpha * image
+        alphas.append(alpha)
 
     for k in range(n_s):
         fin_send[k] = chunk_res[:, k * share : (k + 1) * share]
@@ -270,9 +268,9 @@
 
     each(n_s, lambda j: fin_copy(j, s).start())
     fin_recv[s] = fin_send[s]
-    total_rec = -(alpha * grads[HSTEPS - 1])
-    for step in range(HSTEPS - 1):
-        total_rec = total_rec - grads[step]
+    total_rec = -(alphas[0] * grads[0])
+    for step in range(1, HSTEPS):
+        total_rec = total_rec - alphas[step] * grads[step]
     rec_out[...] = total_rec
 
     def in_done(j):

time: 49.9 us -> 49.4 us (0.990)
  Pallas kernels: 47.8 us -> 47.3 us
    pallas_call x1, Pallas kernels: 47.8 us -> 47.3 us  [shards(): pl.pallas_call(functools.partial(kernel_body, n_s, n_c), out_shape=(pltpu...]
where the time goes in v4:
time: 49.4 us; the launch traced here: 49.2 us
  Pallas kernels  47.3 us (96%)
  local copies, waits for them, and re-layouts  1.27 us (3%)
  between operations  0.64 us (1%)
    pallas_call x1, Pallas kernels, shards(): pl.pallas_call(functools.partial(kernel_body, n_s, n_c), out_shape=(pltpu...  47.3 us
    unnamed x2, local copies, waits for them, and re-layouts  1.27 us

profile of v4, /device:TPU:0, one launch (start us, length us, event | category | flops | bytes accessed | tf_op | source)
XLA Modules:
  0.0 49.2 jit_solution(6836460370294212134)
XLA Ops:
  0.6 47.3 %shard_map.86 = (f32[32,1024]{1,0:T(8,128)S(1)}, f32[64,128]{1,0:T(8,128)S(1)}) custom-call(bf16[8,1024]{1,0:T(8,128)(2,1)} %gs.1, bf16[16,1024]{1,0:T(8,128)(2,1)} %gr.1, s32[1,512]{1,0:T(1,128)} %bitcast.2, s32[1,512]{1,0:T(1,128)} %bitcast.3, s32[1,1024]{1,0:T(1,128)} %order.1, bf16[128,1024]{1,0:T(8,128)(2,1)} %models.1, bf16[512,128]{1,0:T(8,128)(2,1)} %noise.1), custom_call_target="tpu_custom_call" | custom-call | tf_op jit(solution)/shard_map/pallas_call | solution.py:305
  47.9 0.7 %copy.11 = f32[32,1024]{1,0:T(8,128)} copy(f32[32,1024]{1,0:T(8,128)S(1)} %get-tuple-element.2) | data formatting | bytes 262144
  48.6 0.6 %copy.12 = f32[64,128]{1,0:T(8,128)} copy(f32[64,128]{1,0:T(8,128)S(1)} %get-tuple-element.3) | data formatting | bytes 65536
